TPU v7x, 512 devices: a whole 4x8x8 slice. The times are simulated.
512 devices in a mesh: seq: 64 (over y, x, core), fsdp: 8 (over z).
Axes of the slice: x: 4, y: 8, z: 8, core: 2. Of those that a mesh axis runs over, the one named last changes fastest.
Arguments:
- activation_entries: bfloat16 [8192, 4096], P('seq', 'fsdp'), may hold values from -6 to 6
- content_mapping_matrix: bfloat16 [4096, 4096], P('seq', 'fsdp'), may hold values from -0.09375 to 0.09375
- content_lagged_blend: float32 [4096], P('fsdp'), may hold values from 0 to 1
- acceptance_vectors: bfloat16 [8192, 4096], P('seq', 'fsdp'), may hold values from -6 to 6
- address_vectors_given: bfloat16 [8192, 4096], P('seq', 'fsdp'), may hold values from -6 to 6
- inline_adaptation_speed: bfloat16 [8192, 4096], P('seq', 'fsdp'), may hold values from 0 to 1
- memory_fading_factors: float32 [8192, 4096], P('seq', 'fsdp'), may hold values from 0.6 to 1
- result_filter_given: bfloat16 [8192, 4096], P('seq', 'fsdp'), may hold values from 0.099609375 to 1.5
- extra_coordinate_factors: float32 [4096], P('fsdp'), may hold values from -0.75 to 0.75
- group_layernorm_scaling: float32 [4096], P('fsdp'), may hold values from 0.1 to 1.9
- group_layernorm_offset: float32 [4096], P('fsdp'), may hold values from -4 to 4
Outputs:
- time_mix: bfloat16 [8192, 4096], P('seq', 'fsdp')
All inputs are finite; a program needn't handle non-finite values.
Results may differ from a plain program's by a relative error of at most 0.0056.
Values may be sent and summed in bfloat16 or wider, within the bound.
A program may use at most 64 MiB of HBM per device.

v0:
```python
import jax
import jax.numpy as jnp
from jax import lax
from jax.sharding import PartitionSpec as P

GROUP_DIMENSION = 64
norm_eps = 0.00064
unit_eps = 1e-05
highest = lax.Precision.HIGHEST


def shifted_2(value, axis, steps):
    count = lax.axis_size(axis)
    first, last = (max(0, -steps), min(count, count - steps))
    return lax.ppermute(value, axis, [(source, source + steps) for source in range(first, last)])


def prefix_2(value, axis, join, neutral):
    count, mine = (lax.axis_size(axis), lax.axis_index(axis))
    pieces = lax.all_gather(value, axis)
    so_far = jnp.full_like(value, 0) + jnp.asarray(neutral, value.dtype)

    def step(position, so_far):
        longer = join(so_far, pieces[position])
        return jnp.where(position < mine, longer, so_far)

    return lax.fori_loop(0, count - 1, step, so_far)


def shards(
    activation_entries,
    content_mapping_matrix,
    content_lagged_blend,
    acceptance_vectors,
    address_vectors_given,
    inline_adaptation_speed,
    memory_fading_factors,
    result_filter_given,
    extra_coordinate_factors,
    group_layernorm_scaling,
    group_layernorm_offset,
):
    element_matrix_lines, portion_breadth = activation_entries.shape
    resident_groups = portion_breadth // GROUP_DIMENSION
    as_float = activation_entries.astype(jnp.float32)
    previous = shifted_2(activation_entries[-1:, :], "seq", 1)
    shifted = jnp.concatenate([previous.astype(jnp.float32), as_float[:-1]], axis=0)
    mixed = (as_float + (shifted - as_float) * content_lagged_blend[None, :]).astype(jnp.bfloat16)
    columns = lax.all_gather(content_mapping_matrix, "seq", axis=0, tiled=True)
    projected = jnp.dot(
        lax.all_gather(mixed, "fsdp", axis=1, tiled=True),
        columns,
        preferred_element_type=jnp.float32,
    )
    value = projected.astype(jnp.bfloat16)
    block_len = min(128, element_matrix_lines)
    blocks = element_matrix_lines // block_len

    def split_heads(array):
        shaped = array.astype(jnp.float32).reshape(
            blocks, block_len, resident_groups, GROUP_DIMENSION
        )
        return shaped.transpose(0, 2, 1, 3)

    rec_blocks = split_heads(acceptance_vectors)
    key_blocks = split_heads(address_vectors_given)
    rate_blocks = split_heads(inline_adaptation_speed)
    decay_blocks = split_heads(memory_fading_factors)
    value_blocks = split_heads(value)
    unit = key_blocks * lax.rsqrt(
        jnp.sum(key_blocks * key_blocks, axis=-1, keepdims=True) + unit_eps
    )
    cumul = jnp.cumprod(decay_blocks, axis=2)
    cumul_prev = jnp.concatenate([jnp.ones_like(cumul[:, :, :1]), cumul[:, :, :-1]], axis=2)
    cumul_end = cumul[:, :, -1:, :]
    erase_dir = -unit * cumul_prev
    write_dir = unit * rate_blocks / cumul
    key_scaled = key_blocks / cumul
    rec_scaled = rec_blocks * cumul
    strict = jnp.tril(jnp.ones((block_len, block_len), jnp.float32), -1)
    inclusive = jnp.tril(jnp.ones((block_len, block_len), jnp.float32))
    eye_block = jnp.eye(block_len, dtype=jnp.float32)
    erase_write = jnp.einsum("bhck,bhdk->bhcd", erase_dir, write_dir, precision=highest) * strict
    erase_key = jnp.einsum("bhck,bhdk->bhcd", erase_dir, key_scaled, precision=highest) * strict
    read_write = jnp.einsum("bhck,bhdk->bhcd", rec_scaled, write_dir, precision=highest) * inclusive
    read_key = jnp.einsum("bhck,bhdk->bhcd", rec_scaled, key_scaled, precision=highest) * inclusive
    system = eye_block - erase_write
    write_end = write_dir * cumul_end
    key_end = key_scaled * cumul_end

    def run_blocks(initial, values, want_rows):

        def block_step(state, inputs):
            (
                erase_b,
                rec_b,
                system_b,
                erase_key_b,
                read_write_b,
                read_key_b,
                write_e,
                key_e,
                cumul_e,
                value_b,
            ) = inputs
            rhs = jnp.einsum("hck,hrk->hcr", erase_b, state, precision=highest) + jnp.einsum(
                "hcd,hdr->hcr", erase_key_b, value_b, precision=highest
            )
            pseudo = lax.linalg.triangular_solve(
                system_b, rhs, left_side=True, lower=True, unit_diagonal=True
            )
            new_state = (
                state * cumul_e
                + jnp.einsum("hcr,hck->hrk", pseudo, write_e, precision=highest)
                + jnp.einsum("hcr,hck->hrk", value_b, key_e, precision=highest)
            )
            if want_rows:
                out_rows = (
                    jnp.einsum("hck,hrk->hcr", rec_b, state, precision=highest)
                    + jnp.einsum("hcd,hdr->hcr", read_write_b, pseudo, precision=highest)
                    + jnp.einsum("hcd,hdr->hcr", read_key_b, value_b, precision=highest)
                )
                return (new_state, out_rows)
            return (new_state, None)

        inputs = (
            erase_dir,
            rec_scaled,
            system,
            erase_key,
            read_write,
            read_key,
            write_end,
            key_end,
            cumul_end,
            values,
        )
        return lax.scan(block_step, initial, inputs)

    identity_part = jnp.broadcast_to(
        jnp.eye(GROUP_DIMENSION, dtype=jnp.float32),
        (resident_groups, GROUP_DIMENSION, GROUP_DIMENSION),
    )
    zero_part = jnp.zeros((resident_groups, GROUP_DIMENSION, GROUP_DIMENSION), jnp.float32)
    start_aug = jnp.concatenate([zero_part, identity_part], axis=1)
    values_aug = jnp.concatenate([value_blocks, jnp.zeros_like(value_blocks)], axis=-1)
    ends, outs_aug = run_blocks(start_aug, values_aug, False)
    payload = jnp.swapaxes(ends, 1, 2)

    def combine_pairs(earlier, later):
        moved = jnp.einsum(
            "hij,hjr->hir", later[:, :, GROUP_DIMENSION:], earlier, precision=highest
        )
        return moved + jnp.concatenate(
            [later[:, :, :GROUP_DIMENSION], jnp.zeros_like(later[:, :, GROUP_DIMENSION:])], axis=-1
        )

    identity_pair = jnp.concatenate([zero_part, identity_part], axis=-1)
    prefix = prefix_2(payload, "seq", combine_pairs, identity_pair)
    incoming = jnp.swapaxes(prefix[:, :, :GROUP_DIMENSION], 1, 2)
    final_state, read_blocks = run_blocks(incoming, value_blocks, True)
    read = read_blocks.transpose(0, 2, 1, 3).reshape(
        element_matrix_lines, resident_groups, GROUP_DIMENSION
    )
    centre = read - jnp.mean(read, axis=-1, keepdims=True)
    spread = jnp.mean(centre * centre, axis=-1, keepdims=True)
    standardized_result = (centre * lax.rsqrt(spread + norm_eps)).reshape(
        element_matrix_lines, portion_breadth
    ) * group_layernorm_scaling[None, :] + group_layernorm_offset[None, :]
    acceptance_by_group = acceptance_vectors.astype(jnp.float32).reshape(
        element_matrix_lines, resident_groups, GROUP_DIMENSION
    )
    address_by_group = address_vectors_given.astype(jnp.float32).reshape(
        element_matrix_lines, resident_groups, GROUP_DIMENSION
    )
    content_by_group = value.astype(jnp.float32).reshape(
        element_matrix_lines, resident_groups, GROUP_DIMENSION
    )
    scaled_aggregate_figure = jnp.sum(
        acceptance_by_group
        * address_by_group
        * extra_coordinate_factors.reshape(resident_groups, GROUP_DIMENSION)[None],
        axis=-1,
        keepdims=True,
    )
    present_extra_term = (scaled_aggregate_figure * content_by_group).reshape(
        element_matrix_lines, portion_breadth
    )
    return (
        (standardized_result + present_extra_term) * result_filter_given.astype(jnp.float32)
    ).astype(jnp.bfloat16)


def solution(mesh):
    return jax.shard_map(
        shards,
        mesh=mesh,
        in_specs=(
            P("seq", "fsdp"),
            P("seq", "fsdp"),
            P("fsdp"),
            P("seq", "fsdp"),
            P("seq", "fsdp"),
            P("seq", "fsdp"),
            P("seq", "fsdp"),
            P("seq", "fsdp"),
            P("fsdp"),
            P("fsdp"),
            P("fsdp"),
        ),
        out_specs=P("seq", "fsdp"),
        check_vma=False,
    )
```

profile of v0, /device:TPU:1, one launch (start us, length us, event | category | flops | bytes accessed | tf_op | source)
XLA Modules:
  0.0 370.4 jit_solution(16223546304854679737)
XLA Ops:
  7.2 4.5 %collective-permute-start = (bf16[1,512]{1,0:T(2,128)(2,1)S(1)}, bf16[1,512]{1,0:T(2,128)(2,1)S(1)}, u32[]{:S(2)}, u32[]{:S(2)}) collective-permute-start(bf16[1,512]{1,0:T(2,128)(2,1)S(1)} %slice.40), channel_id=1, source_target_pairs={{0,8},{8,16},{16,24},{24,32},{32,40},{40,48},{48,56},{56,64},{64,7... | collective-permute-start | bytes 3080 | tf_op jit(solution)/shard_map/ppermute | solution.py:15
  12.7 3.4 collective-permute-done
  16.0 1.6 fusion.25
  18.5 1.0 copy.54
  19.5 1.1 copy.50
  20.6 1.1 copy.52
  22.0 1.0 copy.56
  23.4 23.3 %fusion.43 = f32[1,8,128,64]{3,1,2,0:T(8,128)S(1)} fusion(f32[1,8,128,64]{3,1,2,0:T(8,128)S(1)} %copy.53), kind=kOutput, calls=%fused_computation.81 | output fusion | flops 8323072 | bytes 524288 | tf_op jit(solution)/shard_map/jit(cumprod)/reduce_window | solution.py:73
  48.0 2.7 multiply_bitcast_fusion.1
  50.7 1.2 copy.58
  51.9 1.2 copy.62
  53.1 1.2 copy.59
  54.6 1.0 fusion.6
  55.6 79.2 %custom-call.7 = f32[8,1,128,128]{2,3,1,0:T(8,128)} custom-call(f32[8,1,128,128]{3,2,1,0:T(8,128)S(1)} %fusion.6), custom_call_target="InvertDiagBlocksLowerTriangular" | custom-call | tf_op jit(solution)/shard_map/while/body/eval_jaxpr/triangular_solve | solution.py:109
  135.5 1.9 fusion.21
  137.4 1.0 convolution_multiply_fusion.2
  138.5 10.8 %all-gather.7.cloned.1.call-done = bf16[4096,512]{1,0:T(8,128)(2,1)} async-done(((bf16[64,512]{1,0:T(8,128)(2,1)}), bf16[4096,512]{1,0:T(8,128)(2,1)}) %all-gather.7.cloned.1.call-update) | async-done | bytes 4194320 | tf_op jit(solution)/shard_map/all_gather | solution.py:49
  149.3 3.2 convolution_convert_fusion
  153.4 1.1 copy.64
  154.5 1.7 convolution_add_fusion.1
  156.2 2.1 fusion.12
  158.3 1.1 convolution_add_fusion.6
  159.4 1.7 fusion.7
  163.9 1.2 copy.70
  165.3 1.0 convolution_multiply_fusion.1
  166.3 1.0 convolution_multiply_fusion
  168.1 96.3 %all-gather.9.cloned.1.call-done = f32[512,64,128]{2,1,0:T(8,128)} async-done(((f32[8,64,128]{2,1,0:T(8,128)}), f32[512,64,128]{2,1,0:T(8,128)}) %all-gather.9.cloned.1.call-update) | async-done | bytes 16777232 | tf_op jit(solution)/shard_map/all_gather | solution.py:20
  264.3 93.2 %while.8 = (s32[]{:T(128)}, f32[8,64,128]{2,1,0:T(8,128)S(1)}, s32[]{:T(128)}, f32[64,8,64,128]{3,2,1,0:T(8,128)}, s32[]{:T(128)}, /*index=5*/pred[128]{0:T(512)(128)(4,1)S(1)}) while((s32[]{:T(128)}, f32[8,64,128]{2,1,0:T(8,128)S(1)}, s32[]{:T(128)}, f32[64,8,64,128]{3,2,1,0:T(8,128)}, s32[]{:T(128)}, ...), condition=%wide.region_3.4_spmd, body=%wide.region_2.3_spmd.sunk | while | flops 50528256 | bytes 2359899 | solution.py:27
  264.4 1.0 dynamic-slice_bitcast_fusion.2
  265.9 1.0 dynamic-slice_bitcast_fusion.2
  267.4 1.0 dynamic-slice_bitcast_fusion.2
  268.9 1.0 dynamic-slice_bitcast_fusion.2
  271.8 1.0 dynamic-slice_bitcast_fusion.2
  273.3 1.0 dynamic-slice_bitcast_fusion.2
  274.8 1.0 dynamic-slice_bitcast_fusion.2
  276.2 1.0 dynamic-slice_bitcast_fusion.2
  277.7 1.0 dynamic-slice_bitcast_fusion.2
  279.2 1.0 dynamic-slice_bitcast_fusion.2
  282.2 1.0 dynamic-slice_bitcast_fusion.2
  285.1 1.0 dynamic-slice_bitcast_fusion.2
  286.6 1.0 dynamic-slice_bitcast_fusion.2
  288.1 1.0 dynamic-slice_bitcast_fusion.2
  289.6 1.0 dynamic-slice_bitcast_fusion.2
  291.0 1.0 dynamic-slice_bitcast_fusion.2
  292.5 1.0 dynamic-slice_bitcast_fusion.2
  295.5 1.0 dynamic-slice_bitcast_fusion.2
  358.6 1.6 convolution_add_fusion.4
  360.8 1.1 convolution_add_fusion.3
  (245 shorter events, 86.3 us)
Async XLA Ops:
  6.5 131.9 %all-gather.5.cloned.1.call-start = ((), (), s32[]{:S(2)}) async-start(), calls=%async_computation | async-start | bytes 1179648 | tf_op jit(solution)/shard_map/all_gather | solution.py:51
  7.2 8.8 %collective-permute-start = (bf16[1,512]{1,0:T(2,128)(2,1)S(1)}, bf16[1,512]{1,0:T(2,128)(2,1)S(1)}, u32[]{:S(2)}, u32[]{:S(2)}) collective-permute-start(bf16[1,512]{1,0:T(2,128)(2,1)S(1)} %slice.40), channel_id=1, source_target_pairs={{0,8},{8,16},{16,24},{24,32},{32,40},{40,48},{48,56},{56,64},{64,7... | collective-permute-start | bytes 3080 | tf_op jit(solution)/shard_map/ppermute | solution.py:15
  17.7 131.6 %all-gather.7.cloned.1.call-start = ((), (), s32[]{:S(2)}) async-start(), calls=%async_computation.1 | async-start | bytes 4259840 | tf_op jit(solution)/shard_map/all_gather | solution.py:49
  18.5 245.9 %all-gather.9.cloned.1.call-start = ((), (), s32[]{:S(2)}) async-start(), calls=%async_computation.2 | async-start | bytes 17039360 | tf_op jit(solution)/shard_map/all_gather | solution.py:20
  19.5 31.2 %copy-start.2 = (bf16[128,512]{0,1:T(8,128)(2,1)}, bf16[128,512]{0,1:T(8,128)(2,1)S(1)}, u32[]{:S(2)}) copy-start(bf16[128,512]{0,1:T(8,128)(2,1)S(1)} %copy.54) | copy-start | bytes 393220
  20.6 30.1 %copy-start.4 = (bf16[128,512]{0,1:T(8,128)(2,1)}, bf16[128,512]{0,1:T(8,128)(2,1)S(1)}, u32[]{:S(2)}) copy-start(bf16[128,512]{0,1:T(8,128)(2,1)S(1)} %copy.50) | copy-start | bytes 393220
  134.8 0.6 copy-start.7
  152.5 9.4 %copy-start.12 = (f32[512]{0:T(512)S(1)}, f32[512]{0:T(512)}, u32[]{:S(2)}) copy-start(f32[512]{0:T(512)} %param.21) | copy-start | bytes 6148
  152.5 9.5 %copy-start.3 = (bf16[128,512]{0,1:T(8,128)(2,1)S(1)}, bf16[128,512]{0,1:T(8,128)(2,1)}, u32[]{:S(2)}) copy-start(bf16[128,512]{0,1:T(8,128)(2,1)} %copy-done.2) | copy-start | bytes 393220
  152.5 9.5 %copy-start.5 = (bf16[128,512]{0,1:T(8,128)(2,1)S(1)}, bf16[128,512]{0,1:T(8,128)(2,1)}, u32[]{:S(2)}) copy-start(bf16[128,512]{0,1:T(8,128)(2,1)} %copy-done.4) | copy-start | bytes 393220
  159.4 105.0 %copy-start.9 = (pred[128]{0:T(512)(128)(4,1)S(1)}, pred[128]{0:T(512)(128)(4,1)}, u32[]{:S(2)}) copy-start(pred[128]{0:T(512)(128)(4,1)} %constant.95.clone.1) | copy-start | bytes 388
  264.3 95.8 %copy-start = (f32[8,1,128,128]{2,3,1,0:T(8,128)S(1)}, f32[8,1,128,128]{2,3,1,0:T(8,128)}, u32[]{:S(2)}) copy-start(f32[8,1,128,128]{2,3,1,0:T(8,128)} %custom-call.7) | copy-start | bytes 1572868
  357.8 4.1 %copy-start.1 = (bf16[128,512]{0,1:T(8,128)(2,1)S(1)}, bf16[128,512]{0,1:T(8,128)(2,1)}, u32[]{:S(2)}) copy-start(bf16[128,512]{0,1:T(8,128)(2,1)} %copy.74) | copy-start | bytes 393220
  357.8 5.3 %copy-start.10 = (f32[512]{0:T(512)S(1)}, f32[512]{0:T(512)}, u32[]{:S(2)}) copy-start(f32[512]{0:T(512)} %param.23) | copy-start | bytes 6148
  357.8 5.3 %copy-start.11 = (f32[512]{0:T(512)S(1)}, f32[512]{0:T(512)}, u32[]{:S(2)}) copy-start(f32[512]{0:T(512)} %param.22) | copy-start | bytes 6148
  358.5 4.6 %copy-start.6 = (f32[128,512]{1,0:T(8,128)S(1)}, f32[128,512]{1,0:T(8,128)}, u32[]{:S(2)}) copy-start(f32[128,512]{1,0:T(8,128)} %copy.81) | copy-start | bytes 786436
  360.2 2.9 copy-start.8
Sparse Core Ops, SparseCore 0:
  17.8 40.1 all-gather.4
  61.4 87.8 all-gather.6
  161.2 103.0 all-gather.8
where the time goes:
time: 373 us; the launch traced here: 370 us
  waiting for transfers between devices  111 us (30%)
  other arithmetic  109 us (29%)
  local copies, waits for them, and re-layouts  81 us (22%)
  matrix products  48.5 us (13%)
  between operations  13.7 us (4%)
  starting transfers between devices  4.58 us (1%)
    all_gather x1, waiting for transfers between devices, prefix_2(): pieces = lax.all_gather(value, axis)  96.3 us
    another operation x4, other arithmetic, block_step(): lax.linalg.triangular_solve(system_b, rhs, left_side=True, lower=True, un...  79.3 us
    squeeze x63, local copies, waits for them, and re-layouts, step(): longer = join(so_far, pieces[position])  61.5 us
    dot_general x63, matrix products, combine_pairs(): jnp.einsum('hij,hjr->hir', later[:, :, GROUP_DIMENSION:], earlier, precis...  28.1 us
    another operation x1, other arithmetic, shards(): cumul = jnp.cumprod(decay_blocks, axis=2)  23.3 us
    all_gather x1, waiting for transfers between devices, shards(): columns = lax.all_gather(content_mapping_matrix, 'seq', axis=0, tiled=True)  10.8 us
  transfers between devices with their start and end apart: 4, of which 3 were waited for; matrix products, arithmetic and copies ran while one was open for 34% of the time, Pallas kernels for 0%

commit v1 on v0

--- a/solution.py
+++ b/solution.py
@@ -46,7 +46,10 @@
     previous = shifted_2(activation_entries[-1:, :], "seq", 1)
     shifted = jnp.concatenate([previous.astype(jnp.float32), as_float[:-1]], axis=0)
     mixed = (as_float + (shifted - as_float) * content_lagged_blend[None, :]).astype(jnp.bfloat16)
-    columns = lax.all_gather(content_mapping_matrix, "seq", axis=0, tiled=True)
+    columns = jnp.concatenate(
+        lax.all_to_all(jnp.stack([content_mapping_matrix] * lax.axis_size("seq")), "seq", 0, 0),
+        axis=0,
+    )
     projected = jnp.dot(
         lax.all_gather(mixed, "fsdp", axis=1, tiled=True),
         columns,

time: 373 us -> 434 us (1.16)
  waiting for transfers between devices: 111 us -> 163 us
  starting transfers between devices: 4.58 us -> 15.8 us
    all_gather x1, waiting for transfers between devices: 96.3 us -> 153 us  [prefix_2(): pieces = lax.all_gather(value, axis)]
    all_to_all x0 -> x1, starting transfers between devices: none -> 12 us  [shards(): lax.all_to_all(jnp.stack([content_mapping_matrix] * lax.axis_size('seq'))...]
    all_gather x1 -> x0, waiting for transfers between devices: 10.8 us -> none  [shards(): columns = lax.all_gather(content_mapping_matrix, 'seq', axis=0, tiled=True)]
    all_gather x1, waiting for transfers between devices: 0.02 us -> 9.86 us  [shards(): lax.all_gather(mixed, 'fsdp', axis=1, tiled=True)]
  transfers between devices with their start and end apart: 4 -> 4, of which waited for: 3 -> 2; matrix products, arithmetic and copies ran while one was open for 34% -> 29% of each run, Pallas kernels for 0% -> 0%
where the time goes in v1:
time: 434 us; the launch traced here: 431 us
  waiting for transfers between devices  163 us (38%)
  other arithmetic  108 us (25%)
  local copies, waits for them, and re-layouts  79 us (18%)
  matrix products  48.5 us (11%)
  starting transfers between devices  15.8 us (4%)
  between operations  14.1 us (3%)
    all_gather x1, waiting for transfers between devices, prefix_2(): pieces = lax.all_gather(value, axis)  153 us
    another operation x4, other arithmetic, block_step(): lax.linalg.triangular_solve(system_b, rhs, left_side=True, lower=True, un...  79.5 us
    squeeze x63, local copies, waits for them, and re-layouts, step(): longer = join(so_far, pieces[position])  61.5 us
    dot_general x63, matrix products, combine_pairs(): jnp.einsum('hij,hjr->hir', later[:, :, GROUP_DIMENSION:], earlier, precis...  28.1 us
    another operation x1, other arithmetic, shards(): cumul = jnp.cumprod(decay_blocks, axis=2)  23.3 us
    all_to_all x1, starting transfers between devices, shards(): lax.all_to_all(jnp.stack([content_mapping_matrix] * lax.axis_size('seq'))...  12 us
    all_gather x1, waiting for transfers between devices, shards(): lax.all_gather(mixed, 'fsdp', axis=1, tiled=True)  9.86 us
  transfers between devices with their start and end apart: 4, of which 2 were waited for; matrix products, arithmetic and copies ran while one was open for 29% of the time, Pallas kernels for 0%

profile of v1, /device:TPU:1, one launch (start us, length us, event | category | flops | bytes accessed | tf_op | source)
XLA Modules:
  0.0 431.1 jit_solution(1245224375036654320)
XLA Ops:
  6.5 3.3 stack.2
  9.9 12.0 %all-to-all-start = ((bf16[64,64,512]{2,1,0:T(8,128)(2,1)}), bf16[64,64,512]{2,1,0:T(8,128)(2,1)}, u32[]{:S(2)}, u32[]{:S(2)}) async-start(bf16[64,64,512]{2,1,0:T(8,128)(2,1)} %stack.2), calls=%async_computation | async-start | bytes 8388608 | tf_op jit(solution)/shard_map/all_to_all | solution.py:50
  22.0 3.7 collective-permute-start
  26.7 23.3 %fusion.43 = f32[1,8,128,64]{3,1,2,0:T(8,128)S(1)} fusion(f32[1,8,128,64]{3,1,2,0:T(8,128)S(1)} %copy.53), kind=kOutput, calls=%fused_computation.81 | output fusion | flops 8323072 | bytes 524288 | tf_op jit(solution)/shard_map/jit(cumprod)/reduce_window | solution.py:76
  52.4 2.6 multiply_bitcast_fusion.1
  55.0 1.2 copy.58
  56.2 1.2 copy.62
  57.5 1.2 copy.59
  58.9 1.0 fusion.6
  59.9 79.4 %custom-call.7 = f32[8,1,128,128]{2,3,1,0:T(8,128)} custom-call(f32[8,1,128,128]{3,2,1,0:T(8,128)S(1)} %fusion.6), custom_call_target="InvertDiagBlocksLowerTriangular" | custom-call | tf_op jit(solution)/shard_map/while/body/eval_jaxpr/triangular_solve | solution.py:112
  140.0 1.9 fusion.21
  141.9 1.0 convolution_multiply_fusion.2
  142.9 9.9 %all-gather.4.cloned.1.call-done = bf16[128,4096]{1,0:T(8,128)(2,1)} async-done(((bf16[128,512]{1,0:T(8,128)(2,1)}), bf16[128,4096]{1,0:T(8,128)(2,1)}) %all-gather.4.cloned.1.call-update) | async-done | bytes 1048592 | tf_op jit(solution)/shard_map/all_gather | solution.py:54
  152.8 3.2 convolution_convert_fusion
  156.8 1.1 copy.64
  158.0 1.7 convolution_add_fusion.1
  159.7 2.1 fusion.12
  161.7 1.1 convolution_add_fusion.6
  162.8 1.7 fusion.7
  167.1 1.2 copy.70
  168.6 1.0 convolution_multiply_fusion.1
  169.6 1.0 convolution_multiply_fusion
  171.3 153.1 %all-gather.6.cloned.1.call-done = f32[512,64,128]{2,1,0:T(8,128)} async-done(((f32[8,64,128]{2,1,0:T(8,128)}), f32[512,64,128]{2,1,0:T(8,128)}) %all-gather.6.cloned.1.call-update) | async-done | bytes 16777232 | tf_op jit(solution)/shard_map/all_gather | solution.py:20
  324.5 93.4 %while.8 = (s32[]{:T(128)}, f32[8,64,128]{2,1,0:T(8,128)S(1)}, s32[]{:T(128)}, f32[64,8,64,128]{3,2,1,0:T(8,128)}, s32[]{:T(128)}, /*index=5*/pred[128]{0:T(512)(128)(4,1)S(1)}) while((s32[]{:T(128)}, f32[8,64,128]{2,1,0:T(8,128)S(1)}, s32[]{:T(128)}, f32[64,8,64,128]{3,2,1,0:T(8,128)}, s32[]{:T(128)}, ...), condition=%wide.region_3.4_spmd, body=%wide.region_2.3_spmd.sunk | while | flops 50528256 | bytes 2359899 | solution.py:27
  324.5 1.0 dynamic-slice_bitcast_fusion.2
  326.0 1.0 dynamic-slice_bitcast_fusion.2
  327.5 1.0 dynamic-slice_bitcast_fusion.2
  330.4 1.0 dynamic-slice_bitcast_fusion.2
  331.9 1.0 dynamic-slice_bitcast_fusion.2
  333.4 1.0 dynamic-slice_bitcast_fusion.2
  334.9 1.0 dynamic-slice_bitcast_fusion.2
  336.4 1.0 dynamic-slice_bitcast_fusion.2
  337.8 1.0 dynamic-slice_bitcast_fusion.2
  339.3 1.0 dynamic-slice_bitcast_fusion.2
  343.8 1.0 dynamic-slice_bitcast_fusion.2
  345.2 1.0 dynamic-slice_bitcast_fusion.2
  346.7 1.0 dynamic-slice_bitcast_fusion.2
  348.2 1.0 dynamic-slice_bitcast_fusion.2
  349.7 1.0 dynamic-slice_bitcast_fusion.2
  351.1 1.0 dynamic-slice_bitcast_fusion.2
  355.6 1.0 dynamic-slice_bitcast_fusion.2
  357.1 1.0 dynamic-slice_bitcast_fusion.2
  358.5 1.0 dynamic-slice_bitcast_fusion.2
  360.0 1.0 dynamic-slice_bitcast_fusion.2
  361.5 1.0 dynamic-slice_bitcast_fusion.2
  363.0 1.0 dynamic-slice_bitcast_fusion.2
  418.9 1.6 convolution_add_fusion.4
  421.1 1.1 convolution_add_fusion.3
  (257 shorter events, 81.1 us)
Async XLA Ops:
  9.9 12.1 %copy-start.1 = (bf16[128,512]{1,0:T(8,128)(2,1)S(1)}, bf16[128,512]{1,0:T(8,128)(2,1)}, u32[]{:S(2)}) copy-start(bf16[128,512]{1,0:T(8,128)(2,1)} %param.13) | copy-start | bytes 393220
  9.9 15.8 %copy-start.10 = (bf16[128,512]{1,0:T(8,128)(2,1)S(1)}, bf16[128,512]{1,0:T(8,128)(2,1)}, u32[]{:S(2)}) copy-start(bf16[128,512]{1,0:T(8,128)(2,1)} %param.17) | copy-start | bytes 393220
  9.9 16.0 %copy-start.9 = (f32[128,512]{1,0:T(8,128)S(1)}, f32[128,512]{1,0:T(8,128)}, u32[]{:S(2)}) copy-start(f32[128,512]{1,0:T(8,128)} %param.19) | copy-start | bytes 786436
  9.9 142.9 %all-to-all-start = ((bf16[64,64,512]{2,1,0:T(8,128)(2,1)}), bf16[64,64,512]{2,1,0:T(8,128)(2,1)}, u32[]{:S(2)}, u32[]{:S(2)}) async-start(bf16[64,64,512]{2,1,0:T(8,128)(2,1)} %stack.2), calls=%async_computation | async-start | bytes 8388608 | tf_op jit(solution)/shard_map/all_to_all | solution.py:50
  21.9 28.2 %copy-start.15 = (f32[512]{0:T(512)S(1)}, f32[512]{0:T(512)}, u32[]{:S(2)}) copy-start(f32[512]{0:T(512)} %param.15) | copy-start | bytes 6148
  21.9 29.8 %copy-start.11 = (bf16[128,512]{1,0:T(8,128)(2,1)S(1)}, bf16[128,512]{1,0:T(8,128)(2,1)}, u32[]{:S(2)}) copy-start(bf16[128,512]{1,0:T(8,128)(2,1)} %param.16) | copy-start | bytes 393220
  21.9 29.9 %copy-start.12 = (bf16[128,512]{1,0:T(8,128)(2,1)S(1)}, bf16[128,512]{1,0:T(8,128)(2,1)}, u32[]{:S(2)}) copy-start(bf16[128,512]{1,0:T(8,128)(2,1)} %param.18) | copy-start | bytes 393220
  21.9 130.8 %all-gather.4.cloned.1.call-start = ((), (), s32[]{:S(2)}) async-start(), calls=%async_computation.1 | async-start | bytes 1179648 | tf_op jit(solution)/shard_map/all_gather | solution.py:54
  22.0 28.1 %collective-permute-start = (bf16[1,512]{1,0:T(2,128)(2,1)S(1)}, bf16[1,512]{1,0:T(2,128)(2,1)S(1)}, u32[]{:S(2)}, u32[]{:S(2)}) collective-permute-start(bf16[1,512]{1,0:T(2,128)(2,1)S(1)} %slice.40), channel_id=1, source_target_pairs={{0,8},{8,16},{16,24},{24,32},{32,40},{40,48},{48,56},{56,64},{64,7... | collective-permute-start | bytes 3080 | tf_op jit(solution)/shard_map/ppermute | solution.py:15
  25.8 0.7 copy-start.3
  50.9 273.6 %all-gather.6.cloned.1.call-start = ((), (), s32[]{:S(2)}) async-start(), calls=%async_computation.2 | async-start | bytes 17039360 | tf_op jit(solution)/shard_map/all_gather | solution.py:20
  51.9 5.6 %copy-start.5 = (bf16[128,512]{0,1:T(8,128)(2,1)}, bf16[128,512]{0,1:T(8,128)(2,1)S(1)}, u32[]{:S(2)}) copy-start(bf16[128,512]{0,1:T(8,128)(2,1)S(1)} %copy.50) | copy-start | bytes 393220
  139.4 0.6 copy-start.8
  156.0 9.4 %copy-start.18 = (f32[512]{0:T(512)S(1)}, f32[512]{0:T(512)}, u32[]{:S(2)}) copy-start(f32[512]{0:T(512)} %param.21) | copy-start | bytes 6148
  156.0 9.5 %copy-start.4 = (bf16[128,512]{0,1:T(8,128)(2,1)S(1)}, bf16[128,512]{0,1:T(8,128)(2,1)}, u32[]{:S(2)}) copy-start(bf16[128,512]{0,1:T(8,128)(2,1)} %copy-done.3) | copy-start | bytes 393220
  156.0 9.5 %copy-start.6 = (bf16[128,512]{0,1:T(8,128)(2,1)S(1)}, bf16[128,512]{0,1:T(8,128)(2,1)}, u32[]{:S(2)}) copy-start(bf16[128,512]{0,1:T(8,128)(2,1)} %copy-done.5) | copy-start | bytes 393220
  162.8 161.6 %copy-start.14 = (pred[128]{0:T(512)(128)(4,1)S(1)}, pred[128]{0:T(512)(128)(4,1)}, u32[]{:S(2)}) copy-start(pred[128]{0:T(512)(128)(4,1)} %constant.95.clone.1) | copy-start | bytes 388
  324.5 96.0 %copy-start = (f32[8,1,128,128]{2,3,1,0:T(8,128)S(1)}, f32[8,1,128,128]{2,3,1,0:T(8,128)}, u32[]{:S(2)}) copy-start(f32[8,1,128,128]{2,3,1,0:T(8,128)} %custom-call.7) | copy-start | bytes 1572868
  418.1 4.1 copy-start.2
  418.1 5.3 %copy-start.16 = (f32[512]{0:T(512)S(1)}, f32[512]{0:T(512)}, u32[]{:S(2)}) copy-start(f32[512]{0:T(512)} %param.23) | copy-start | bytes 6148
  418.1 5.3 %copy-start.17 = (f32[512]{0:T(512)S(1)}, f32[512]{0:T(512)}, u32[]{:S(2)}) copy-start(f32[512]{0:T(512)} %param.22) | copy-start | bytes 6148
  418.9 4.6 %copy-start.7 = (f32[128,512]{1,0:T(8,128)S(1)}, f32[128,512]{1,0:T(8,128)}, u32[]{:S(2)}) copy-start(f32[128,512]{1,0:T(8,128)} %copy.81) | copy-start | bytes 786436
  420.5 3.0 copy-start.13
Sparse Core Ops, SparseCore 0:
  51.0 101.7 all-gather.3
  164.7 159.7 all-gather.5
